TPU v7x, 32 devices: a whole 2x2x4 slice. The times are simulated.
32 devices in a mesh: animal: 8 (over z, y), snp: 4 (over x, core).
Axes of the slice: x: 2, y: 2, z: 4, core: 2. Of those that a mesh axis runs over, the one named last changes fastest.
Arguments:
- genotype: bfloat16 [8192, 32768], P('animal', 'snp')
- allele_freq: float32 [32768], P('snp')
- right_side: float32 [8192, 128], P('animal'), may hold values from -6 to 6
- diagonal: float32 [8192, 128], P('animal'), may hold values from 0.5 to 2
- mendelian: float32 [8192], P('animal'), may hold values from 2 to 4
- genomic_weight: float32 [128], replicated, may hold values from 1 to 8
- send_rows: int32 [8, 8, 64], P('animal'), may hold values from 0 to 1023, as said below
- sire_slot: int32 [8192], P('animal'), may hold values from 0 to 463, as said below
- dam_slot: int32 [8192], P('animal'), may hold values from 16 to 511, as said below
Outputs:
- solution: float32 [8192, 128], P('animal')
- residual: float32 [8192, 128], P('animal')
Inputs may be any that keep to these rules, and one draw needn't show every extreme that they name: send_rows[o, d, :] lists 64 distinct local rows of owner o's 1024 animals, those sent to device d. sire_slot[i] = o * 64 + k with k < 16. dam_slot[i] = o * 64 + k with k >= 16.
All inputs are finite; a program needn't handle non-finite values.
Results may differ from a plain program's by a relative error of at most 0.0067.
Values may be sent and summed in bfloat16 or wider, within the bound.
No kernel may reach another device: no remote copies, remote signals or barrier semaphores. Data moves between devices by JAX's collectives and lax.ppermute only.
A program may use at most 64 MiB of HBM per device.

v0:
```python
import jax
import jax.numpy as jnp
from jax import lax
from jax.sharding import PartitionSpec as P

SNPS = 32768
ITERS = 2


def local(
    genotype,
    allele_freq,
    right_side,
    diagonal,
    mendelian,
    genomic_weight,
    send_rows,
    sire_slot,
    dam_slot,
):
    owners = lax.axis_size("animal")
    slots = send_rows.shape[2]
    centered = (genotype.astype(jnp.float32) - 2.0 * allele_freq[None, :]).astype(jnp.bfloat16)
    outgoing_rows = send_rows[0]
    flat_rows = outgoing_rows.reshape(-1)
    scale = genomic_weight[None, :] / SNPS

    def pedigree(field):
        width = field.shape[1]
        outgoing = field[outgoing_rows]
        incoming = lax.all_to_all(outgoing, "animal", split_axis=0, concat_axis=0, tiled=True)
        received = incoming.reshape(owners * slots, width)
        mendel_term = mendelian[:, None] * (
            field - 0.5 * (received[sire_slot] + received[dam_slot])
        )
        back = jnp.zeros((owners * slots, width), jnp.float32)
        back = back.at[sire_slot].add(-0.5 * mendel_term).at[dam_slot].add(-0.5 * mendel_term)
        returned = lax.all_to_all(
            back.reshape(owners, slots, width), "animal", split_axis=0, concat_axis=0, tiled=True
        )
        return mendel_term + jnp.zeros_like(field).at[flat_rows].add(returned.reshape(-1, width))

    def genomic(field):
        field_b = field.astype(jnp.bfloat16)
        block = centered
        owned = lax.psum_scatter(
            lax.dot_general(
                block, field_b, (((0,), (0,)), ((), ())), preferred_element_type=jnp.float32
            ),
            "animal",
            scatter_dimension=0,
            tiled=True,
        )
        owned_b = owned.astype(jnp.bfloat16)
        block = centered
        partial_value = jnp.dot(
            block,
            lax.all_gather(owned_b, "animal", axis=0, tiled=True),
            preferred_element_type=jnp.float32,
        )
        return lax.psum(partial_value, "snp")

    def operate(field):
        ped = pedigree(field)
        return diagonal * field + ped + scale * genomic(field)

    solution = jnp.zeros_like(right_side)
    residual = right_side
    w_field = operate(residual)
    z_field = jnp.zeros_like(right_side)
    s_field = jnp.zeros_like(right_side)
    p_field = jnp.zeros_like(right_side)
    gamma_prev = None
    alpha_prev = None
    for step in range(ITERS):
        gamma, delta = lax.psum(
            (jnp.sum(residual * residual, axis=0), jnp.sum(w_field * residual, axis=0)), "animal"
        )
        q_field = operate(w_field)
        if step == 0:
            beta = jnp.zeros_like(gamma)
            alpha = gamma / delta
        else:
            beta = gamma / gamma_prev
            alpha = gamma / (delta - beta * gamma / alpha_prev)
        z_field = q_field + beta * z_field
        s_field = w_field + beta * s_field
        p_field = residual + beta * p_field
        solution = solution + alpha * p_field
        residual = residual - alpha * s_field
        w_field = w_field - alpha * z_field
        gamma_prev = gamma
        alpha_prev = alpha
    return (solution, residual)


def solution(mesh):
    placed = (
        P("animal", "snp"),
        P("snp"),
        P("animal", None),
        P("animal", None),
        P("animal"),
        P(),
        P("animal", None, None),
        P("animal"),
        P("animal"),
    )
    return jax.shard_map(
        local,
        mesh=mesh,
        in_specs=placed,
        out_specs=(P("animal", None), P("animal", None)),
        check_vma=False,
    )
```

profile of v0, /device:TPU:0, one launch (start us, length us, event | category | flops | bytes accessed | tf_op | source)
XLA Modules:
  0.0 508.4 jit_solution(10293679810259572106)
XLA Ops:
  7.2 0.0 reduce-scatter.3.cloned.1.call-start
  7.2 0.8 broadcast_multiply_fusion
  8.0 12.8 %fusion.3 = f32[8192,128]{1,0:T(8,128)} fusion(bf16[1024,8192]{1,0:T(8,128)(2,1)} %param.9, f32[8192]{0:T(1024)S(1)} %broadcast_multiply_fusion, f32[1024,128]{1,0:T(8,128)} %param.11), kind=kOutput, calls=%fused_computation.16 | convolution fusion | flops 2172780544 | bytes 21528576 | tf_op jit(solution)/shard_map/dot_general | solution.py:47
  20.8 0.0 reduce-scatter.3.cloned.1.call-update
  20.9 0.0 all-gather.3.cloned.1.call-start
  20.9 91.2 %reduce-scatter.3.cloned.1.call-done = f32[1024,128]{1,0:T(8,128)} async-done(((f32[8192,128]{1,0:T(8,128)}), f32[1024,128]{1,0:T(8,128)}) %reduce-scatter.3.cloned.1.call-update) | async-done | bytes 524304 | tf_op jit(solution)/shard_map/reduce_scatter | solution.py:46
  112.1 1.8 convert_element_type.21
  113.8 0.0 all-gather.3.cloned.1.call-update
  113.9 0.1 reshape.94
  114.0 1.6 gather_fusion
  115.6 4.2 all-to-all-start
  119.8 0.2 all-reduce.5.cloned.1.call-start
  120.1 45.6 %all-gather.3.cloned.1.call-done = bf16[8192,128]{1,0:T(8,128)(2,1)} async-done(((bf16[1024,128]{1,0:T(8,128)(2,1)}), bf16[8192,128]{1,0:T(8,128)(2,1)}) %all-gather.3.cloned.1.call-update) | async-done | bytes 2097168 | tf_op jit(solution)/shard_map/all_gather | solution.py:58
  165.7 11.7 %fusion.2 = f32[1024,128]{1,0:T(8,128)} fusion(bf16[8192,128]{1,0:T(8,128)(2,1)} %all-gather.3.cloned.1.call-done, bf16[1024,8192]{1,0:T(8,128)(2,1)} %param.9, f32[8192]{0:T(1024)S(1)} %broadcast_multiply_fusion), kind=kOutput, calls=%fused_computation.15 | convolution fusion | flops 2172649472 | bytes 19431424 | tf_op jit(solution)/shard_map/dot_general | solution.py:56
  177.4 0.0 all-reduce.5.cloned.1.call-update
  177.5 2.8 gather_fusion.1
  180.3 2.8 gather_fusion.2
  183.1 26.3 %all-reduce.5.cloned.1.call-done = f32[1024,128]{1,0:T(8,128)} async-done(((f32[1024,128]{1,0:T(8,128)}), f32[1024,128]{1,0:T(8,128)}) %all-reduce.5.cloned.1.call-update) | async-done | bytes 524304 | tf_op jit(solution)/shard_map/psum | solution.py:61
  209.5 1.2 multiply_add_fusion.2
  210.7 6.7 %scatter_custom_fusion = f32[512,128]{1,0:T(8,128)} fusion(s32[1024]{0:T(1024)S(1)} %get-tuple-element.22, f32[1024,128]{1,0:T(8,128)S(1)} %get-tuple-element.15, f32[]{:T(128)} %constant.3.clone.1, f32[]{:T(128)} %constant.8.clone.1), kind=kCustom, calls=%fused_computation.35 | custom fusion | flops 262144 | bytes 786440 | tf_op jit(solution)/shard_map/scatter-add | solution.py:37
  217.4 7.1 %scatter_custom_fusion.1 = f32[512,128]{1,0:T(8,128)} fusion(f32[512,128]{1,0:T(8,128)} %scatter_custom_fusion, s32[1024]{0:T(1024)S(1)} %get-tuple-element.20, f32[1024,128]{1,0:T(8,128)S(1)} %get-tuple-element.15, f32[]{:T(128)} %constant.3.clone.1), kind=kCustom, calls=%fused_computation.33 | custom fusion | flops 262144 | bytes 786944 | tf_op jit(solution)/shard_map/scatter-add | solution.py:37
  224.6 5.5 %all-to-all-start.1 = ((f32[8,64,128]{2,1,0:T(8,128)}), f32[8,64,128]{2,1,0:T(8,128)S(1)}, u32[]{:S(2)}, u32[]{:S(2)}) async-start(f32[8,64,128]{2,1,0:T(8,128)} %bitcast.4), calls=%async_computation.2 | async-start | bytes 524288 | tf_op jit(solution)/shard_map/all_to_all | solution.py:38
  230.1 0.0 reduce-scatter.5.cloned.1.call-start
  230.1 0.1 reshape_squeeze.3
  230.2 8.1 %all-to-all-done.1 = f32[8,64,128]{2,1,0:T(8,128)S(1)} async-done(((f32[8,64,128]{2,1,0:T(8,128)}), f32[8,64,128]{2,1,0:T(8,128)S(1)}, u32[]{:S(2)}, u32[]{:S(2)}) %all-to-all-start.1) | async-done | bytes 262176 | tf_op jit(solution)/shard_map/all_to_all | solution.py:38
  238.3 3.7 scatter_fusion
  242.0 10.5 %fusion.1 = f32[8192,128]{1,0:T(8,128)} fusion(bf16[1024,8192]{1,0:T(8,128)(2,1)} %param.9, f32[8192]{0:T(1024)S(1)} %broadcast_multiply_fusion, f32[1024,128]{1,0:T(8,128)S(1)} %scatter_fusion), kind=kOutput, calls=%fused_computation.14 | convolution fusion | flops 2172780544 | bytes 21528576 | tf_op jit(solution)/shard_map/dot_general | solution.py:47
  252.5 0.0 all-gather.5.cloned.1.call-start
  252.6 86.7 %reduce-scatter.5.cloned.1.call-done = f32[1024,128]{1,0:T(8,128)} async-done(((f32[8192,128]{1,0:T(8,128)}), f32[1024,128]{1,0:T(8,128)}) %reduce-scatter.5.cloned.1.call-update) | async-done | bytes 524304 | tf_op jit(solution)/shard_map/reduce_scatter | solution.py:46
  339.3 1.8 convert_element_type.23
  341.1 1.6 gather_fusion.3
  342.7 4.2 all-to-all-start.2
  347.0 0.0 all-reduce.7.cloned.1.call-start
  347.0 45.8 %all-gather.5.cloned.1.call-done = bf16[8192,128]{1,0:T(8,128)(2,1)} async-done(((bf16[1024,128]{1,0:T(8,128)(2,1)}), bf16[8192,128]{1,0:T(8,128)(2,1)}) %all-gather.5.cloned.1.call-update) | async-done | bytes 2097168 | tf_op jit(solution)/shard_map/all_gather | solution.py:58
  392.8 11.7 %fusion = f32[1024,128]{1,0:T(8,128)} fusion(bf16[8192,128]{1,0:T(8,128)(2,1)} %all-gather.5.cloned.1.call-done, bf16[1024,8192]{1,0:T(8,128)(2,1)} %param.9, f32[8192]{0:T(1024)S(1)} %broadcast_multiply_fusion), kind=kOutput, calls=%fused_computation.13 | convolution fusion | flops 2172649472 | bytes 19431424 | tf_op jit(solution)/shard_map/dot_general | solution.py:56
  404.5 0.0 all-reduce.7.cloned.1.call-update
  404.5 2.8 gather_fusion.4
  407.3 4.0 gather_fusion.5
  411.4 25.2 %all-reduce.7.cloned.1.call-done = f32[1024,128]{1,0:T(8,128)} async-done(((f32[1024,128]{1,0:T(8,128)}), f32[1024,128]{1,0:T(8,128)}) %all-reduce.7.cloned.1.call-update) | async-done | bytes 524304 | tf_op jit(solution)/shard_map/psum | solution.py:61
  436.6 1.5 multiply_reduce_fusion.2
  438.1 6.7 %scatter_custom_fusion.3 = f32[512,128]{1,0:T(8,128)} fusion(s32[1024]{0:T(1024)S(1)} %get-tuple-element.22, f32[1024,128]{1,0:T(8,128)S(1)} %get-tuple-element.19, f32[]{:T(128)} %constant.3.clone.1, f32[]{:T(128)} %constant.8.clone.1), kind=kCustom, calls=%fused_computation.31 | custom fusion | flops 262144 | bytes 786440 | tf_op jit(solution)/shard_map/scatter-add | solution.py:37
  444.8 7.1 %scatter_custom_fusion.4 = f32[512,128]{1,0:T(8,128)} fusion(f32[512,128]{1,0:T(8,128)} %scatter_custom_fusion.3, s32[1024]{0:T(1024)S(1)} %get-tuple-element.20, f32[1024,128]{1,0:T(8,128)S(1)} %get-tuple-element.19, f32[]{:T(128)} %constant.3.clone.1), kind=kCustom, calls=%fused_computation.29 | custom fusion | flops 262144 | bytes 786944 | tf_op jit(solution)/shard_map/scatter-add | solution.py:37
  451.9 5.5 %all-to-all-start.3 = ((f32[8,64,128]{2,1,0:T(8,128)}), f32[8,64,128]{2,1,0:T(8,128)S(1)}, u32[]{:S(2)}, u32[]{:S(2)}) async-start(f32[8,64,128]{2,1,0:T(8,128)} %bitcast.8), calls=%async_computation.5 | async-start | bytes 524288 | tf_op jit(solution)/shard_map/all_to_all | solution.py:38
  457.4 21.8 %all-reduce.1 = (f32[128]{0:T(128)S(1)}, f32[128]{0:T(128)S(1)}) all-reduce(f32[128]{0:T(128)S(1)} %get-tuple-element.5, f32[128]{0:T(128)S(1)} %get-tuple-element.4), channel_id=1, replica_groups=mesh['animal'=8,'snp'=4] {'animal'}, use_global_device_ids=true, to_apply=%region_1.0 | all-reduce | flops 256 | bytes 2048 | tf_op jit(solution)/shard_map/psum | solution.py:76
  479.2 3.8 scatter_fusion.1
  483.0 0.2 multiply_reduce_fusion
  483.2 17.1 %all-reduce = (f32[128]{0:T(128)S(1)}, f32[128]{0:T(128)S(1)}) all-reduce(f32[128]{0:T(128)S(1)} %get-tuple-element.3, f32[128]{0:T(128)S(1)} %get-tuple-element.2), channel_id=1, replica_groups=mesh['animal'=8,'snp'=4] {'animal'}, use_global_device_ids=true, to_apply=%region_10.0 | all-reduce | flops 256 | bytes 2048 | tf_op jit(solution)/shard_map/psum | solution.py:76
  500.3 1.2 multiply_subtract_fusion
  (27 shorter events, 0.1 us)
Async XLA Ops:
  7.2 104.9 %reduce-scatter.3.cloned.1.call-start = ((), (), s32[]{:S(2)}) async-start(), calls=%async_computation.6 | async-start | bytes 4718592 | tf_op jit(solution)/shard_map/reduce_scatter | solution.py:46
  8.0 105.9 %copy-start.2 = (s32[1,8,64]{2,1,0:T(8,128)S(1)}, s32[1,8,64]{2,1,0:T(8,128)}, u32[]{:S(2)}) copy-start(s32[1,8,64]{2,1,0:T(8,128)} %param.15) | copy-start | bytes 6148
  8.0 106.0 %copy-start = (f32[1024,128]{1,0:T(8,128)S(1)}, f32[1024,128]{1,0:T(8,128)}, u32[]{:S(2)}) copy-start(f32[1024,128]{1,0:T(8,128)} %param.11) | copy-start | bytes 1572868
  8.0 112.1 %copy-start.4 = (s32[1024]{0:T(1024)S(1)}, s32[1024]{0:T(1024)}, u32[]{:S(2)}) copy-start(s32[1024]{0:T(1024)} %param.16) | copy-start | bytes 12292
  20.9 144.9 %all-gather.3.cloned.1.call-start = ((), (), s32[]{:S(2)}) async-start(), calls=%async_computation.7 | async-start | bytes 2359296 | tf_op jit(solution)/shard_map/all_gather | solution.py:58
  115.6 61.9 %all-to-all-start = ((f32[8,64,128]{2,1,0:T(8,128)}), f32[8,64,128]{2,1,0:T(8,128)S(1)}, u32[]{:S(2)}, u32[]{:S(2)}) async-start(f32[8,64,128]{2,1,0:T(8,128)} %bitcast.1), calls=%async_computation | async-start | bytes 524288 | tf_op jit(solution)/shard_map/all_to_all | solution.py:31
  119.8 89.6 %all-reduce.5.cloned.1.call-start = ((), (), s32[]{:S(2)}) async-start(), calls=%async_computation.8 | async-start | bytes 1048576 | tf_op jit(solution)/shard_map/psum | solution.py:61
  120.1 57.3 %copy-start.6 = (f32[128]{0:T(128)S(1)}, f32[128]{0:T(128)}, u32[]{:S(2)}) copy-start(f32[128]{0:T(128)} %param.14) | copy-start | bytes 1540
  120.1 57.3 %copy-start.5 = (s32[1024]{0:T(1024)S(1)}, s32[1024]{0:T(1024)}, u32[]{:S(2)}) copy-start(s32[1024]{0:T(1024)} %param.17) | copy-start | bytes 12292
  120.1 89.3 %copy-start.1 = (f32[1024,128]{1,0:T(8,128)S(1)}, f32[1024,128]{1,0:T(8,128)}, u32[]{:S(2)}) copy-start(f32[1024,128]{1,0:T(8,128)} %param.12) | copy-start | bytes 1572868
  120.1 89.3 %copy-start.3 = (f32[1024]{0:T(1024)S(1)}, f32[1024]{0:T(1024)}, u32[]{:S(2)}) copy-start(f32[1024]{0:T(1024)} %param.13) | copy-start | bytes 12292
  224.6 13.7 %all-to-all-start.1 = ((f32[8,64,128]{2,1,0:T(8,128)}), f32[8,64,128]{2,1,0:T(8,128)S(1)}, u32[]{:S(2)}, u32[]{:S(2)}) async-start(f32[8,64,128]{2,1,0:T(8,128)} %bitcast.4), calls=%async_computation.2 | async-start | bytes 524288 | tf_op jit(solution)/shard_map/all_to_all | solution.py:38
  230.1 109.2 %reduce-scatter.5.cloned.1.call-start = ((), (), s32[]{:S(2)}) async-start(), calls=%async_computation.9 | async-start | bytes 4718592 | tf_op jit(solution)/shard_map/reduce_scatter | solution.py:46
  252.5 140.3 %all-gather.5.cloned.1.call-start = ((), (), s32[]{:S(2)}) async-start(), calls=%async_computation.10 | async-start | bytes 2359296 | tf_op jit(solution)/shard_map/all_gather | solution.py:58
  342.7 61.8 %all-to-all-start.2 = ((f32[8,64,128]{2,1,0:T(8,128)}), f32[8,64,128]{2,1,0:T(8,128)S(1)}, u32[]{:S(2)}, u32[]{:S(2)}) async-start(f32[8,64,128]{2,1,0:T(8,128)} %bitcast.6), calls=%async_computation.3 | async-start | bytes 524288 | tf_op jit(solution)/shard_map/all_to_all | solution.py:31
  347.0 89.7 %all-reduce.7.cloned.1.call-start = ((), (), s32[]{:S(2)}) async-start(), calls=%async_computation.11 | async-start | bytes 1048576 | tf_op jit(solution)/shard_map/psum | solution.py:61
  451.9 27.3 %all-to-all-start.3 = ((f32[8,64,128]{2,1,0:T(8,128)}), f32[8,64,128]{2,1,0:T(8,128)S(1)}, u32[]{:S(2)}, u32[]{:S(2)}) async-start(f32[8,64,128]{2,1,0:T(8,128)} %bitcast.8), calls=%async_computation.5 | async-start | bytes 524288 | tf_op jit(solution)/shard_map/all_to_all | solution.py:38
Sparse Core Ops, SparseCore 0:
  21.0 91.0 reduce-scatter.2
  114.8 50.9 all-gather.2
  177.5 31.8 all-reduce.4
  252.6 86.5 reduce-scatter.4
  341.8 50.9 all-gather.4
  404.6 31.9 all-reduce.6
where the time goes:
time: 509 us; the launch traced here: 508 us
  waiting for transfers between devices  329 us (65%)
  matrix products  46.6 us (9%)
  other arithmetic  43.6 us (9%)
  blocking collectives  39 us (8%)
  starting transfers between devices  19.9 us (4%)
  local copies, waits for them, and re-layouts  16 us (3%)
  between operations  14.3 us (3%)
    reduce_scatter x2, waiting for transfers between devices, genomic(): lax.psum_scatter(lax.dot_general(block, field_b, (((0,), (0,)), ((), ()))...  178 us
    all_gather x2, waiting for transfers between devices, genomic(): lax.all_gather(owned_b, 'animal', axis=0, tiled=True)  91.4 us
    psum x2, waiting for transfers between devices, genomic(): return lax.psum(partial_value, 'snp')  51.6 us
    psum x2, blocking collectives, local(): lax.psum((jnp.sum(residual * residual, axis=0), jnp.sum(w_field * residua...  39 us
    scatter-add x4, other arithmetic, pedigree(): back.at[sire_slot].add(-0.5 * mendel_term).at[dam_slot]  27.7 us
    dot_general x2, matrix products, genomic(): jnp.dot(block, lax.all_gather(owned_b, 'animal', axis=0, tiled=True), pre...  23.3 us
    dot_general x2, matrix products, genomic(): lax.dot_general(block, field_b, (((0,), (0,)), ((), ())), preferred_eleme...  23.3 us
    all_to_all x2, starting transfers between devices, pedigree(): lax.all_to_all(back.reshape(owners, slots, width), 'animal', split_axis=0...  11 us
  transfers between devices with their start and end apart: 10, of which 7 were waited for; matrix products, arithmetic and copies ran while one was open for 8% of the time, Pallas kernels for 0%

commit v1 on v0

--- a/solution.py
+++ b/solution.py
@@ -1,3 +1,4 @@
+import functools
 import jax
 import jax.numpy as jnp
 from jax import lax
@@ -5,6 +6,13 @@
 
 SNPS = 32768
 ITERS = 2
+
+
+def tell_sections_for(inputs, axis_id):
+    return lax.all_gather(inputs, axis_id).sum(axis=0)
+
+
+derive_zone = functools.partial(tell_sections_for, axis_id="snp")
 
 
 def local(
@@ -58,7 +66,7 @@
             lax.all_gather(owned_b, "animal", axis=0, tiled=True),
             preferred_element_type=jnp.float32,
         )
-        return lax.psum(partial_value, "snp")
+        return derive_zone(partial_value)
 
     def operate(field):
         ped = pedigree(field)

time: 509 us -> 487 us (0.957)
  waiting for transfers between devices: 329 us -> 295 us
  blocking collectives: 39 us -> 50.4 us
    psum x2 -> x0, waiting for transfers between devices: 51.6 us -> none  [genomic(): return lax.psum(partial_value, 'snp')]
    all_to_all x0 -> x1, blocking collectives: none -> 11.4 us  [pedigree(): lax.all_to_all(outgoing, 'animal', split_axis=0, concat_axis=0, tiled=True)]
    all_to_all x2 -> x1, waiting for transfers between devices: 0.01 us -> 7.93 us  [pedigree(): lax.all_to_all(outgoing, 'animal', split_axis=0, concat_axis=0, tiled=True)]
    all_gather x2, waiting for transfers between devices: 91.4 us -> 98.8 us  [genomic(): lax.all_gather(owned_b, 'animal', axis=0, tiled=True)]
  transfers between devices with their start and end apart: 10 -> 9, of which waited for: 7 -> 8; matrix products, arithmetic and copies ran while one was open for 8% -> 4% of each run, Pallas kernels for 0% -> 0%
where the time goes in v1:
time: 487 us; the launch traced here: 486 us
  waiting for transfers between devices  295 us (61%)
  blocking collectives  50.4 us (10%)
  other arithmetic  46.6 us (10%)
  matrix products  46.6 us (10%)
  local copies, waits for them, and re-layouts  17.7 us (4%)
  starting transfers between devices  15.1 us (3%)
  between operations  14.3 us (3%)
    reduce_scatter x2, waiting for transfers between devices, genomic(): lax.psum_scatter(lax.dot_general(block, field_b, (((0,), (0,)), ((), ()))...  178 us
    all_gather x2, waiting for transfers between devices, genomic(): lax.all_gather(owned_b, 'animal', axis=0, tiled=True)  98.8 us
    psum x2, blocking collectives, local(): lax.psum((jnp.sum(residual * residual, axis=0), jnp.sum(w_field * residua...  39 us
    scatter-add x4, other arithmetic, pedigree(): back.at[sire_slot].add(-0.5 * mendel_term).at[dam_slot]  27.7 us
    dot_general x2, matrix products, genomic(): jnp.dot(block, lax.all_gather(owned_b, 'animal', axis=0, tiled=True), pre...  23.3 us
    dot_general x2, matrix products, genomic(): lax.dot_general(block, field_b, (((0,), (0,)), ((), ())), preferred_eleme...  23.3 us
    all_to_all x1, blocking collectives, pedigree(): lax.all_to_all(outgoing, 'animal', split_axis=0, concat_axis=0, tiled=True)  11.4 us
    all_to_all x2, starting transfers between devices, pedigree(): lax.all_to_all(back.reshape(owners, slots, width), 'animal', split_axis=0...  11 us
  transfers between devices with their start and end apart: 9, of which 8 were waited for; matrix products, arithmetic and copies ran while one was open for 4% of the time, Pallas kernels for 0%

profile of v1, /device:TPU:0, one launch (start us, length us, event | category | flops | bytes accessed | tf_op | source)
XLA Modules:
  0.0 486.2 jit_solution(1548471708739226769)
XLA Ops:
  7.2 0.0 reduce-scatter.3.cloned.1.call-start
  7.2 0.8 broadcast_multiply_fusion
  8.0 12.8 %fusion.3 = f32[8192,128]{1,0:T(8,128)} fusion(bf16[1024,8192]{1,0:T(8,128)(2,1)} %param.9, f32[8192]{0:T(1024)S(1)} %broadcast_multiply_fusion, f32[1024,128]{1,0:T(8,128)} %param.11), kind=kOutput, calls=%fused_computation.16 | convolution fusion | flops 2172780544 | bytes 21528576 | tf_op jit(solution)/shard_map/dot_general | solution.py:55
  20.8 0.0 reduce-scatter.3.cloned.1.call-update
  20.8 0.0 all-gather.7.cloned.1.call-start
  20.8 91.2 %reduce-scatter.3.cloned.1.call-done = f32[1024,128]{1,0:T(8,128)} async-done(((f32[8192,128]{1,0:T(8,128)}), f32[1024,128]{1,0:T(8,128)}) %reduce-scatter.3.cloned.1.call-update) | async-done | bytes 524304 | tf_op jit(solution)/shard_map/reduce_scatter | solution.py:54
  112.0 1.8 convert_element_type.21
  113.9 0.0 all-gather.11.cloned.1.call-start
  113.9 49.5 %all-gather.7.cloned.1.call-done = bf16[8192,128]{1,0:T(8,128)(2,1)} async-done(((bf16[1024,128]{1,0:T(8,128)(2,1)}), bf16[8192,128]{1,0:T(8,128)(2,1)}) %all-gather.7.cloned.1.call-update) | async-done | bytes 2097168 | tf_op jit(solution)/shard_map/all_gather | solution.py:66
  163.5 11.7 %fusion.2 = f32[1024,128]{1,0:T(8,128)} fusion(bf16[8192,128]{1,0:T(8,128)(2,1)} %all-gather.7.cloned.1.call-done, bf16[1024,8192]{1,0:T(8,128)(2,1)} %param.9, f32[8192]{0:T(1024)S(1)} %broadcast_multiply_fusion), kind=kOutput, calls=%fused_computation.15 | convolution fusion | flops 2172649472 | bytes 19431424 | tf_op jit(solution)/shard_map/dot_general | solution.py:64
  175.2 0.1 reshape.94
  175.3 1.6 gather_fusion
  176.9 3.6 all-to-all-start
  180.6 7.9 %all-to-all-done = f32[8,64,128]{2,1,0:T(8,128)S(1)} async-done(((f32[8,64,128]{2,1,0:T(8,128)}), f32[8,64,128]{2,1,0:T(8,128)S(1)}, u32[]{:S(2)}, u32[]{:S(2)}) %all-to-all-start) | async-done | bytes 262176 | tf_op jit(solution)/shard_map/all_to_all | solution.py:39
  188.5 2.8 gather_fusion.1
  191.3 4.0 gather_fusion.2
  195.4 1.0 all-gather.11.cloned.1.call-done
  196.4 1.8 reduce_sum.55
  198.2 1.2 multiply_add_fusion.2
  199.4 6.7 %scatter_custom_fusion = f32[512,128]{1,0:T(8,128)} fusion(s32[1024]{0:T(1024)S(1)} %get-tuple-element.22, f32[1024,128]{1,0:T(8,128)S(1)} %get-tuple-element.15, f32[]{:T(128)} %constant.3.clone.1, f32[]{:T(128)} %constant.8.clone.1), kind=kCustom, calls=%fused_computation.35 | custom fusion | flops 262144 | bytes 786440 | tf_op jit(solution)/shard_map/scatter-add | solution.py:45
  206.2 7.1 %scatter_custom_fusion.1 = f32[512,128]{1,0:T(8,128)} fusion(f32[512,128]{1,0:T(8,128)} %scatter_custom_fusion, s32[1024]{0:T(1024)S(1)} %get-tuple-element.20, f32[1024,128]{1,0:T(8,128)S(1)} %get-tuple-element.15, f32[]{:T(128)} %constant.3.clone.1), kind=kCustom, calls=%fused_computation.33 | custom fusion | flops 262144 | bytes 786944 | tf_op jit(solution)/shard_map/scatter-add | solution.py:45
  213.3 5.5 %all-to-all-start.1 = ((f32[8,64,128]{2,1,0:T(8,128)}), f32[8,64,128]{2,1,0:T(8,128)S(1)}, u32[]{:S(2)}, u32[]{:S(2)}) async-start(f32[8,64,128]{2,1,0:T(8,128)} %bitcast.5), calls=%async_computation.2 | async-start | bytes 524288 | tf_op jit(solution)/shard_map/all_to_all | solution.py:46
  218.8 0.0 reduce-scatter.5.cloned.1.call-start
  218.8 0.1 reshape_squeeze.3
  218.9 9.2 %all-to-all-done.1 = f32[8,64,128]{2,1,0:T(8,128)S(1)} async-done(((f32[8,64,128]{2,1,0:T(8,128)}), f32[8,64,128]{2,1,0:T(8,128)S(1)}, u32[]{:S(2)}, u32[]{:S(2)}) %all-to-all-start.1) | async-done | bytes 262176 | tf_op jit(solution)/shard_map/all_to_all | solution.py:46
  228.1 3.5 scatter_fusion
  231.6 10.5 %fusion.1 = f32[8192,128]{1,0:T(8,128)} fusion(bf16[1024,8192]{1,0:T(8,128)(2,1)} %param.9, f32[8192]{0:T(1024)S(1)} %broadcast_multiply_fusion, f32[1024,128]{1,0:T(8,128)S(1)} %scatter_fusion), kind=kOutput, calls=%fused_computation.14 | convolution fusion | flops 2172780544 | bytes 21528576 | tf_op jit(solution)/shard_map/dot_general | solution.py:55
  242.1 0.0 all-gather.9.cloned.1.call-start
  242.1 86.5 %reduce-scatter.5.cloned.1.call-done = f32[1024,128]{1,0:T(8,128)} async-done(((f32[8192,128]{1,0:T(8,128)}), f32[1024,128]{1,0:T(8,128)}) %reduce-scatter.5.cloned.1.call-update) | async-done | bytes 524304 | tf_op jit(solution)/shard_map/reduce_scatter | solution.py:54
  328.6 1.8 convert_element_type.23
  330.4 0.3 all-gather.13.cloned.1.call-start
  330.7 49.3 %all-gather.9.cloned.1.call-done = bf16[8192,128]{1,0:T(8,128)(2,1)} async-done(((bf16[1024,128]{1,0:T(8,128)(2,1)}), bf16[8192,128]{1,0:T(8,128)(2,1)}) %all-gather.9.cloned.1.call-update) | async-done | bytes 2097168 | tf_op jit(solution)/shard_map/all_gather | solution.py:66
  379.9 11.7 %fusion = f32[1024,128]{1,0:T(8,128)} fusion(bf16[8192,128]{1,0:T(8,128)(2,1)} %all-gather.9.cloned.1.call-done, bf16[1024,8192]{1,0:T(8,128)(2,1)} %param.9, f32[8192]{0:T(1024)S(1)} %broadcast_multiply_fusion), kind=kOutput, calls=%fused_computation.13 | convolution fusion | flops 2172649472 | bytes 19431424 | tf_op jit(solution)/shard_map/dot_general | solution.py:64
  391.6 1.0 gather_fusion.3
  392.7 11.4 %all_to_all.20 = f32[8,64,128]{2,1,0:T(8,128)S(1)} all-to-all(f32[8,64,128]{2,1,0:T(8,128)S(1)} %bitcast.25), channel_id=1, replica_groups=mesh['animal'=8,'snp'=4] {'animal'}, dimensions={0} | all-to-all | bytes 524288 | tf_op jit(solution)/shard_map/all_to_all | solution.py:39
  404.1 4.0 gather_fusion.4
  408.1 4.0 gather_fusion.5
  412.1 0.8 all-gather.13.cloned.1.call-done
  412.9 1.8 reduce_sum.58
  414.7 1.5 multiply_reduce_fusion.2
  416.1 6.7 %scatter_custom_fusion.3 = f32[512,128]{1,0:T(8,128)} fusion(s32[1024]{0:T(1024)S(1)} %get-tuple-element.22, f32[1024,128]{1,0:T(8,128)S(1)} %get-tuple-element.19, f32[]{:T(128)} %constant.3.clone.1, f32[]{:T(128)} %constant.8.clone.1), kind=kCustom, calls=%fused_computation.31 | custom fusion | flops 262144 | bytes 786440 | tf_op jit(solution)/shard_map/scatter-add | solution.py:45
  422.8 7.1 %scatter_custom_fusion.4 = f32[512,128]{1,0:T(8,128)} fusion(f32[512,128]{1,0:T(8,128)} %scatter_custom_fusion.3, s32[1024]{0:T(1024)S(1)} %get-tuple-element.20, f32[1024,128]{1,0:T(8,128)S(1)} %get-tuple-element.19, f32[]{:T(128)} %constant.3.clone.1), kind=kCustom, calls=%fused_computation.29 | custom fusion | flops 262144 | bytes 786944 | tf_op jit(solution)/shard_map/scatter-add | solution.py:45
  429.9 5.5 %all-to-all-start.3 = ((f32[8,64,128]{2,1,0:T(8,128)}), f32[8,64,128]{2,1,0:T(8,128)S(1)}, u32[]{:S(2)}, u32[]{:S(2)}) async-start(f32[8,64,128]{2,1,0:T(8,128)} %bitcast.10), calls=%async_computation.5 | async-start | bytes 524288 | tf_op jit(solution)/shard_map/all_to_all | solution.py:46
  435.5 21.8 %all-reduce.1 = (f32[128]{0:T(128)S(1)}, f32[128]{0:T(128)S(1)}) all-reduce(f32[128]{0:T(128)S(1)} %get-tuple-element.5, f32[128]{0:T(128)S(1)} %get-tuple-element.4), channel_id=1, replica_groups=mesh['animal'=8,'snp'=4] {'animal'}, use_global_device_ids=true, to_apply=%region_1.0 | all-reduce | flops 256 | bytes 2048 | tf_op jit(solution)/shard_map/psum | solution.py:84
  457.3 3.5 scatter_fusion.1
  460.8 0.2 multiply_reduce_fusion
  461.0 17.1 %all-reduce = (f32[128]{0:T(128)S(1)}, f32[128]{0:T(128)S(1)}) all-reduce(f32[128]{0:T(128)S(1)} %get-tuple-element.3, f32[128]{0:T(128)S(1)} %get-tuple-element.2), channel_id=1, replica_groups=mesh['animal'=8,'snp'=4] {'animal'}, use_global_device_ids=true, to_apply=%region_10.0 | all-reduce | flops 256 | bytes 2048 | tf_op jit(solution)/shard_map/psum | solution.py:84
  478.1 1.2 multiply_subtract_fusion
  (28 shorter events, 0.2 us)
Async XLA Ops:
  7.2 104.8 %reduce-scatter.3.cloned.1.call-start = ((), (), s32[]{:S(2)}) async-start(), calls=%async_computation.6 | async-start | bytes 4718592 | tf_op jit(solution)/shard_map/reduce_scatter | solution.py:54
  20.8 142.7 %all-gather.7.cloned.1.call-start = ((), (), s32[]{:S(2)}) async-start(), calls=%async_computation.7 | async-start | bytes 2359296 | tf_op jit(solution)/shard_map/all_gather | solution.py:66
  113.8 61.4 %copy-start.2 = (s32[1,8,64]{2,1,0:T(8,128)S(1)}, s32[1,8,64]{2,1,0:T(8,128)}, u32[]{:S(2)}) copy-start(s32[1,8,64]{2,1,0:T(8,128)} %param.15) | copy-start | bytes 6148
  113.8 61.5 %copy-start = (f32[1024,128]{1,0:T(8,128)S(1)}, f32[1024,128]{1,0:T(8,128)}, u32[]{:S(2)}) copy-start(f32[1024,128]{1,0:T(8,128)} %param.11) | copy-start | bytes 1572868
  113.8 66.7 %copy-start.6 = (f32[128]{0:T(128)S(1)}, f32[128]{0:T(128)}, u32[]{:S(2)}) copy-start(f32[128]{0:T(128)} %param.14) | copy-start | bytes 1540
  113.8 66.7 %copy-start.4 = (s32[1024]{0:T(1024)S(1)}, s32[1024]{0:T(1024)}, u32[]{:S(2)}) copy-start(s32[1024]{0:T(1024)} %param.16) | copy-start | bytes 12292
  113.8 66.7 %copy-start.5 = (s32[1024]{0:T(1024)S(1)}, s32[1024]{0:T(1024)}, u32[]{:S(2)}) copy-start(s32[1024]{0:T(1024)} %param.17) | copy-start | bytes 12292
  113.8 84.3 %copy-start.1 = (f32[1024,128]{1,0:T(8,128)S(1)}, f32[1024,128]{1,0:T(8,128)}, u32[]{:S(2)}) copy-start(f32[1024,128]{1,0:T(8,128)} %param.12) | copy-start | bytes 1572868
  113.9 84.3 %copy-start.3 = (f32[1024]{0:T(1024)S(1)}, f32[1024]{0:T(1024)}, u32[]{:S(2)}) copy-start(f32[1024]{0:T(1024)} %param.13) | copy-start | bytes 12292
  113.9 82.5 %all-gather.11.cloned.1.call-start = ((), (), s32[]{:S(2)}) async-start(), calls=%async_computation.10 | async-start | bytes 2621440 | tf_op jit(solution)/shard_map/all_gather | solution.py:12
  176.9 11.6 %all-to-all-start = ((f32[8,64,128]{2,1,0:T(8,128)}), f32[8,64,128]{2,1,0:T(8,128)S(1)}, u32[]{:S(2)}, u32[]{:S(2)}) async-start(f32[8,64,128]{2,1,0:T(8,128)} %bitcast.1), calls=%async_computation | async-start | bytes 524288 | tf_op jit(solution)/shard_map/all_to_all | solution.py:39
  213.3 14.8 %all-to-all-start.1 = ((f32[8,64,128]{2,1,0:T(8,128)}), f32[8,64,128]{2,1,0:T(8,128)S(1)}, u32[]{:S(2)}, u32[]{:S(2)}) async-start(f32[8,64,128]{2,1,0:T(8,128)} %bitcast.5), calls=%async_computation.2 | async-start | bytes 524288 | tf_op jit(solution)/shard_map/all_to_all | solution.py:46
  218.8 109.8 %reduce-scatter.5.cloned.1.call-start = ((), (), s32[]{:S(2)}) async-start(), calls=%async_computation.8 | async-start | bytes 4718592 | tf_op jit(solution)/shard_map/reduce_scatter | solution.py:54
  242.1 137.9 %all-gather.9.cloned.1.call-start = ((), (), s32[]{:S(2)}) async-start(), calls=%async_computation.9 | async-start | bytes 2359296 | tf_op jit(solution)/shard_map/all_gather | solution.py:66
  330.4 82.5 %all-gather.13.cloned.1.call-start = ((), (), s32[]{:S(2)}) async-start(), calls=%async_computation.11 | async-start | bytes 2621440 | tf_op jit(solution)/shard_map/all_gather | solution.py:12
  429.9 27.3 %all-to-all-start.3 = ((f32[8,64,128]{2,1,0:T(8,128)}), f32[8,64,128]{2,1,0:T(8,128)S(1)}, u32[]{:S(2)}, u32[]{:S(2)}) async-start(f32[8,64,128]{2,1,0:T(8,128)} %bitcast.10), calls=%async_computation.5 | async-start | bytes 524288 | tf_op jit(solution)/shard_map/all_to_all | solution.py:46
Sparse Core Ops, SparseCore 0:
  20.9 91.0 reduce-scatter.2
  114.7 48.7 all-gather.6
  175.3 21.0 all-gather.10
  242.2 86.3 reduce-scatter.4
  331.2 48.7 all-gather.8
  391.8 21.0 all-gather.12
